TPU v7x, 32 devices: a whole 2x2x4 slice. The times are simulated.
32 devices in a mesh: dp: 4 (over z), row: 2 (over x), col: 4 (over y, core).
Axes of the slice: x: 2, y: 2, z: 4, core: 2. Of those that a mesh axis runs over, the one named last changes fastest.
Arguments:
- inputs: bfloat16 [4096, 1024], P(('dp', 'col'), 'row'), may hold values from -12 to 12
- qkv_weight: bfloat16 [1024, 3, 1024], P('row', None, 'col'), may hold values from -10 to 10
- qv_bias: float32 [2, 1024], P(None, 'col'), may hold values from -3 to 3
- out_weight: bfloat16 [1024, 1024], P('col', 'row'), may hold values from -1 to 1
- out_bias: float32 [1024], P('row'), may hold values from -3 to 3
- first_gain: float32 [1024], P('row'), may hold values from 0.1 to 1.9
- first_shift: float32 [1024], P('row'), may hold values from -3 to 3
- up_weight: bfloat16 [1024, 4096], P('row', 'col'), may hold values from -0.1875 to 0.1875
- up_bias: float32 [4096], P('col'), may hold values from -3 to 3
- down_weight: bfloat16 [4096, 1024], P('col', 'row'), may hold values from -0.09375 to 0.09375
- down_bias: float32 [1024], P('row'), may hold values from -3 to 3
- second_gain: float32 [1024], P('row'), may hold values from 0.1 to 1.9
- second_shift: float32 [1024], P('row'), may hold values from -3 to 3
- lengths: int32 [8], P(('dp', 'row')), may hold values from 128 to 512, as said below
- out_grad: bfloat16 [4096, 1024], P(('dp', 'col'), 'row'), may hold values from -9 to 9
Outputs:
- block_out: bfloat16 [4096, 1024], P(('dp', 'col'), 'row')
- grad_inputs: float32 [4096, 1024], P(('dp', 'col'), 'row')
- grad_qkv_weight: float32 [1024, 3, 1024], P('row', None, 'col')
- grad_qv_bias: float32 [2, 1024], P(None, 'col')
- grad_out_weight: float32 [1024, 1024], P('col', 'row')
- grad_out_bias: float32 [1024], P('row')
- grad_first_gain: float32 [1024], P('row')
- grad_first_shift: float32 [1024], P('row')
- grad_up_weight: float32 [1024, 4096], P('row', 'col')
- grad_up_bias: float32 [4096], P('col')
- grad_down_weight: float32 [4096, 1024], P('col', 'row')
- grad_down_bias: float32 [1024], P('row')
- grad_second_gain: float32 [1024], P('row')
- grad_second_shift: float32 [1024], P('row')
Inputs may be any that keep to these rules, and one draw needn't show every extreme that they name: `lengths`: positions at or past a sequence's length are padding.
All inputs are finite; a program needn't handle non-finite values.
Results may differ from a plain program's by a relative error of at most 0.013.
The roundings to bfloat16 on the way count: a program that leaves them out, or rounds other values in their place, can miss the bound.
Values may be sent and summed in bfloat16 or wider, within the bound.
A program may use at most 128 MiB of HBM per device.

v0:
```python
import jax
import jax.numpy as jnp
from jax import lax
from jax.sharding import PartitionSpec as P

MODEL_WIDTH = 1024
HEADS = 16
HEAD_DIM = 64
L = 512
norm_epsilon = 1e-12
masked_score = -1e30
root_half = 0.7071067811865476
gauss_height = 0.3989422804014327


def forward_gather(block):
    return lax.all_gather(block, "col", axis=0, tiled=True)


def forward_reduce(product_term, row_count):
    return lax.psum_scatter(
        product_term(jnp.int32(0), row_count * lax.axis_size("row")),
        "row",
        scatter_dimension=0,
        tiled=True,
    )


def forward_collect(block):
    return lax.all_gather(block, "row", axis=0, tiled=True)


def forward_combine(product_term, row_count):
    return lax.psum_scatter(
        product_term(jnp.int32(0), row_count * lax.axis_size("col")),
        "col",
        scatter_dimension=0,
        tiled=True,
    )


def backward_gather(block):
    return lax.all_gather(block, "col", axis=0, tiled=True)


def backward_reduce(product_term, row_count):
    return lax.psum_scatter(
        product_term(jnp.int32(0), row_count * lax.axis_size("row")),
        "row",
        scatter_dimension=0,
        tiled=True,
    )


def backward_collect(block):
    return lax.all_gather(block, "row", axis=0, tiled=True)


def backward_combine(product_term, row_count):
    return lax.psum_scatter(
        product_term(jnp.int32(0), row_count * lax.axis_size("col")),
        "col",
        scatter_dimension=0,
        tiled=True,
    )


def width_pair(first_part, second_part):
    return lax.psum((first_part, second_part), "row")


def rows_times(gathered, weight):

    def product_term(first_row, row_count):
        return jnp.dot(gathered, weight, preferred_element_type=jnp.float32)

    return product_term


def rows_times_turned(gathered, weight):

    def product_term(first_row, row_count):
        return lax.dot_general(
            gathered, weight, (((1,), (1,)), ((), ())), preferred_element_type=jnp.float32
        )

    return product_term


def contract_rows(first_side, second_side):
    return lax.dot_general(
        first_side, second_side, (((0,), (0,)), ((), ())), preferred_element_type=jnp.float32
    )


def gelu_pair(preact):
    lower_mass = 0.5 * (1.0 + lax.erf(preact * root_half))
    return (
        preact * lower_mass,
        lower_mass + preact * jnp.exp(-0.5 * preact * preact) * gauss_height,
    )


def norm_forward(hidden, norm_gain, norm_shift):
    center, square = width_pair(
        jnp.sum(hidden, axis=-1, keepdims=True), jnp.sum(hidden * hidden, axis=-1, keepdims=True)
    )
    center = center / MODEL_WIDTH
    square = square / MODEL_WIDTH
    rscale = lax.rsqrt(square - center * center + norm_epsilon)
    normed = (hidden - center) * rscale
    return (normed * norm_gain + norm_shift, normed, rscale)


def norm_back(incoming_gradient, normed, rscale, norm_gain):
    scaled = incoming_gradient * norm_gain
    first_mean, second_mean = width_pair(
        jnp.sum(scaled, axis=-1, keepdims=True), jnp.sum(scaled * normed, axis=-1, keepdims=True)
    )
    return rscale * (scaled - first_mean / MODEL_WIDTH - normed * (second_mean / MODEL_WIDTH))


def score_block(queries, keys_low, lengths):
    scores = jnp.einsum(
        "sqhd,skhd->shqk", queries, keys_low, preferred_element_type=jnp.float32
    ) * HEAD_DIM ** (-0.5)
    visible = lax.broadcasted_iota(jnp.int32, (1, 1, 1, L), 3) < lengths[:, None, None, None]
    return jnp.where(visible, scores, masked_score)


def attend(queries, keys_low, values, lengths):
    scores = score_block(queries, keys_low, lengths)
    row_peak = jnp.max(scores, axis=3, keepdims=True)
    logsum = row_peak + jnp.log(jnp.sum(jnp.exp(scores - row_peak), axis=3, keepdims=True))
    soft_weights = jnp.exp(scores - logsum).astype(jnp.bfloat16)
    attention_output = jnp.einsum(
        "shqk,skhd->sqhd", soft_weights, values, preferred_element_type=jnp.float32
    )
    return (attention_output.astype(jnp.bfloat16), logsum)


def attend_back(queries, keys_low, values, logsum, incoming_gradient, lengths):
    scores = score_block(queries, keys_low, lengths)
    soft_weights = jnp.exp(scores - logsum)
    grad_weights = jnp.einsum(
        "sqhd,skhd->shqk", incoming_gradient, values, preferred_element_type=jnp.float32
    )
    row_inner = jnp.sum(soft_weights * grad_weights, axis=3, keepdims=True)
    score_grad = (soft_weights * (grad_weights - row_inner)).astype(jnp.bfloat16)
    score_scale = HEAD_DIM ** (-0.5)
    grad_queries = (
        jnp.einsum("shqk,skhd->sqhd", score_grad, keys_low, preferred_element_type=jnp.float32)
        * score_scale
    )
    grad_keys = (
        jnp.einsum("shqk,sqhd->skhd", score_grad, queries, preferred_element_type=jnp.float32)
        * score_scale
    )
    grad_values = jnp.einsum(
        "shqk,sqhd->skhd",
        soft_weights.astype(jnp.bfloat16),
        incoming_gradient,
        preferred_element_type=jnp.float32,
    )
    return (grad_queries, grad_keys, grad_values)


def shards(
    inputs,
    qkv_weight,
    qv_bias,
    out_weight,
    out_bias,
    first_gain,
    first_shift,
    up_weight,
    up_bias,
    down_weight,
    down_bias,
    second_gain,
    second_shift,
    lengths,
    out_grad,
):
    head_local = HEADS // lax.axis_size("col")
    seq_local = lengths.shape[0]
    head_shape = (seq_local, L, head_local, HEAD_DIM)
    qkv_flat = qkv_weight.reshape(qkv_weight.shape[0], -1)
    across_rows = inputs.shape[0]
    gathered_in = forward_gather(inputs)
    down_rows = gathered_in.shape[0] // lax.axis_size("row")
    projected = forward_reduce(rows_times(gathered_in, qkv_flat), down_rows).reshape(
        down_rows, 3, -1
    )
    queries = (projected[:, 0] + qv_bias[0]).astype(jnp.bfloat16).reshape(head_shape)
    keys_low = projected[:, 1].astype(jnp.bfloat16).reshape(head_shape)
    values = (projected[:, 2] + qv_bias[1]).astype(jnp.bfloat16).reshape(head_shape)
    attention_output, logsum = attend(queries, keys_low, values, lengths)
    gathered_att = forward_collect(attention_output.reshape(down_rows, -1))
    first_sum = (
        inputs.astype(jnp.float32)
        + forward_combine(rows_times(gathered_att, out_weight), across_rows)
        + out_bias
    )
    first_norm, first_standardized, first_scale = norm_forward(first_sum, first_gain, first_shift)
    gathered_norm = forward_gather(first_norm.astype(jnp.bfloat16))
    preact = forward_reduce(rows_times(gathered_norm, up_weight), down_rows) + up_bias
    activated, gelu_slope = gelu_pair(preact)
    gathered_act = forward_collect(activated.astype(jnp.bfloat16))
    second_sum = (
        first_norm + forward_combine(rows_times(gathered_act, down_weight), across_rows) + down_bias
    )
    second_norm, second_standardized, second_scale = norm_forward(
        second_sum, second_gain, second_shift
    )
    block_out = second_norm.astype(jnp.bfloat16)
    incoming_gradient = out_grad.astype(jnp.float32)
    second_norm_gradient = norm_back(
        incoming_gradient, second_standardized, second_scale, second_gain
    )
    gathered_grad = backward_gather(second_norm_gradient.astype(jnp.bfloat16))
    grad_down = contract_rows(gathered_act, gathered_grad)
    preactivation_gradient = (
        backward_reduce(rows_times_turned(gathered_grad, down_weight), down_rows) * gelu_slope
    )
    gathered_pre = backward_collect(preactivation_gradient.astype(jnp.bfloat16))
    grad_up = contract_rows(gathered_norm, gathered_pre)
    norm_gradient_total = second_norm_gradient + backward_combine(
        rows_times_turned(gathered_pre, up_weight), across_rows
    )
    first_norm_gradient = norm_back(
        norm_gradient_total, first_standardized, first_scale, first_gain
    )
    gathered_first = backward_gather(first_norm_gradient.astype(jnp.bfloat16))
    grad_out = contract_rows(gathered_att, gathered_first)
    attended_grad = (
        backward_reduce(rows_times_turned(gathered_first, out_weight), down_rows)
        .astype(jnp.bfloat16)
        .reshape(head_shape)
    )
    grad_queries, grad_keys, grad_values = attend_back(
        queries, keys_low, values, logsum, attended_grad, lengths
    )
    query_rows_flattened = grad_queries.reshape(down_rows, -1)
    value_rows_flattened = grad_values.reshape(down_rows, -1)
    combined_heads = (
        jnp.stack(
            [query_rows_flattened, grad_keys.reshape(down_rows, -1), value_rows_flattened], axis=1
        )
        .astype(jnp.bfloat16)
        .reshape(down_rows, -1)
    )
    gathered_joined = backward_collect(combined_heads)
    grad_qkv = contract_rows(gathered_in, gathered_joined).reshape(qkv_weight.shape)
    grad_inputs = first_norm_gradient + backward_combine(
        rows_times_turned(gathered_joined, qkv_flat), across_rows
    )
    column_sums = lax.psum(
        (
            jnp.sum(first_norm_gradient, axis=0),
            jnp.sum(norm_gradient_total * first_standardized, axis=0),
            jnp.sum(norm_gradient_total, axis=0),
            jnp.sum(second_norm_gradient, axis=0),
            jnp.sum(incoming_gradient * second_standardized, axis=0),
            jnp.sum(incoming_gradient, axis=0),
        ),
        ("dp", "col"),
    )
    row_sums = lax.psum(
        (
            jnp.stack(
                [jnp.sum(query_rows_flattened, axis=0), jnp.sum(value_rows_flattened, axis=0)]
            ),
            jnp.sum(preactivation_gradient, axis=0),
        ),
        ("dp", "row"),
    )
    grad_qkv, grad_out, grad_up, grad_down = (
        lax.psum(grad_qkv.astype(jnp.bfloat16), "dp").astype(jnp.float32),
        lax.psum(grad_out.astype(jnp.bfloat16), "dp").astype(jnp.float32),
        lax.psum(grad_up.astype(jnp.bfloat16), "dp").astype(jnp.float32),
        lax.psum(grad_down.astype(jnp.bfloat16), "dp").astype(jnp.float32),
    )
    return (
        block_out,
        grad_inputs,
        grad_qkv,
        row_sums[0],
        grad_out,
        column_sums[0],
        column_sums[1],
        column_sums[2],
        grad_up,
        row_sums[1],
        grad_down,
        column_sums[3],
        column_sums[4],
        column_sums[5],
    )


def solution(mesh):
    in_specs = (
        P(("dp", "col"), "row"),
        P("row", None, "col"),
        P(None, "col"),
        P("col", "row"),
        P("row"),
        P("row"),
        P("row"),
        P("row", "col"),
        P("col"),
        P("col", "row"),
        P("row"),
        P("row"),
        P("row"),
        P(("dp", "row")),
        P(("dp", "col"), "row"),
    )
    out_specs = (
        P(("dp", "col"), "row"),
        P(("dp", "col"), "row"),
        P("row", None, "col"),
        P(None, "col"),
        P("col", "row"),
        P("row"),
        P("row"),
        P("row"),
        P("row", "col"),
        P("col"),
        P("col", "row"),
        P("row"),
        P("row"),
        P("row"),
    )
    return jax.shard_map(shards, mesh=mesh, in_specs=in_specs, out_specs=out_specs, check_vma=False)
```

profile of v0, /device:TPU:0, one launch (start us, length us, event | category | flops | bytes accessed | tf_op | source)
XLA Modules:
  0.0 701.3 jit_solution(1587023572651374637)
XLA Ops:
  9.4 19.6 %all-gather.8.cloned.1.call-done = bf16[1024,512]{1,0:T(8,128)(2,1)} async-done(((bf16[256,512]{1,0:T(8,128)(2,1)}), bf16[1024,512]{1,0:T(8,128)(2,1)}) %all-gather.8.cloned.1.call-update) | async-done | bytes 1048592 | tf_op jit(solution)/shard_map/all_gather | solution.py:17
  29.0 3.9 fusion.29
  33.9 42.7 %reduce-scatter.9.cloned.1.call-done = f32[512,768]{1,0:T(8,128)} async-done(((f32[1024,768]{1,0:T(8,128)}), f32[512,768]{1,0:T(8,128)}) %reduce-scatter.9.cloned.1.call-update) | async-done | bytes 1572880 | tf_op jit(solution)/shard_map/reduce_scatter | solution.py:21
  83.1 8.5 %all_gather.25 = bf16[1024,256]{0,1:T(8,128)(2,1)S(1)} all-gather(bf16[512,256]{0,1:T(8,128)(2,1)S(1)} %bitcast.93), channel_id=1, replica_groups=mesh['dp'=4,'row'=2,'col'=4] {'row'}, dimensions={0}, use_global_device_ids=true | all-gather | bytes 786432 | tf_op jit(solution)/shard_map/all_gather | solution.py:30
  94.3 31.3 %reduce-scatter.11.cloned.1.call-done = f32[256,512]{1,0:T(8,128)} async-done(((f32[1024,512]{1,0:T(8,128)}), f32[256,512]{1,0:T(8,128)}) %reduce-scatter.11.cloned.1.call-update) | async-done | bytes 524304 | tf_op jit(solution)/shard_map/reduce_scatter | solution.py:34
  127.6 4.9 all-reduce.5
  134.5 16.8 %all-gather.10.cloned.1.call-done = bf16[1024,512]{1,0:T(8,128)(2,1)} async-done(((bf16[256,512]{1,0:T(8,128)(2,1)}), bf16[1024,512]{1,0:T(8,128)(2,1)}) %all-gather.10.cloned.1.call-update) | async-done | bytes 1048592 | tf_op jit(solution)/shard_map/all_gather | solution.py:17
  151.3 4.8 fusion.31
  156.1 54.5 %reduce-scatter.13.cloned.1.call-done = f32[512,1024]{1,0:T(8,128)} async-done(((f32[1024,1024]{1,0:T(8,128)}), f32[512,1024]{1,0:T(8,128)}) %reduce-scatter.13.cloned.1.call-update) | async-done | bytes 2097168 | tf_op jit(solution)/shard_map/reduce_scatter | solution.py:21
  210.6 3.0 multiply_convert_fusion.1
  213.7 33.2 %all-gather.12.cloned.1.call-done = bf16[1024,1024]{1,0:T(8,128)(2,1)} async-done(((bf16[512,1024]{1,0:T(8,128)(2,1)}), bf16[1024,1024]{1,0:T(8,128)(2,1)}) %all-gather.12.cloned.1.call-update) | async-done | bytes 2097168 | tf_op jit(solution)/shard_map/all_gather | solution.py:30
  246.9 4.2 fusion.32
  251.1 31.3 %reduce-scatter.15.cloned.1.call-done = f32[256,512]{1,0:T(8,128)} async-done(((f32[1024,512]{1,0:T(8,128)}), f32[256,512]{1,0:T(8,128)}) %reduce-scatter.15.cloned.1.call-update) | async-done | bytes 524304 | tf_op jit(solution)/shard_map/reduce_scatter | solution.py:34
  284.6 4.9 all-reduce.4
  291.0 4.9 all-reduce.3
  299.6 16.8 %all-gather.14.cloned.1.call-done = bf16[1024,512]{1,0:T(8,128)(2,1)} async-done(((bf16[256,512]{1,0:T(8,128)(2,1)}), bf16[1024,512]{1,0:T(8,128)(2,1)}) %all-gather.14.cloned.1.call-update) | async-done | bytes 1048592 | tf_op jit(solution)/shard_map/all_gather | solution.py:43
  316.4 4.5 fusion.33
  321.0 54.5 %reduce-scatter.17.cloned.1.call-done = f32[512,1024]{1,0:T(8,128)} async-done(((f32[1024,1024]{1,0:T(8,128)}), f32[512,1024]{1,0:T(8,128)}) %reduce-scatter.17.cloned.1.call-update) | async-done | bytes 2097168 | tf_op jit(solution)/shard_map/reduce_scatter | solution.py:47
  375.5 3.5 fusion.24
  379.2 33.0 %all-gather.16.cloned.1.call-done = bf16[1024,1024]{1,0:T(8,128)(2,1)} async-done(((bf16[512,1024]{1,0:T(8,128)(2,1)}), bf16[1024,1024]{1,0:T(8,128)(2,1)}) %all-gather.16.cloned.1.call-update) | async-done | bytes 2097168 | tf_op jit(solution)/shard_map/all_gather | solution.py:56
  412.2 4.2 fusion.34
  416.5 31.3 %reduce-scatter.19.cloned.1.call-done = f32[256,512]{1,0:T(8,128)} async-done(((f32[1024,512]{1,0:T(8,128)}), f32[256,512]{1,0:T(8,128)}) %reduce-scatter.19.cloned.1.call-update) | async-done | bytes 524304 | tf_op jit(solution)/shard_map/reduce_scatter | solution.py:60
  449.8 4.9 all-reduce.2
  456.9 16.8 %all-gather.18.cloned.1.call-done = bf16[1024,512]{1,0:T(8,128)(2,1)} async-done(((bf16[256,512]{1,0:T(8,128)(2,1)}), bf16[1024,512]{1,0:T(8,128)(2,1)}) %all-gather.18.cloned.1.call-update) | async-done | bytes 1048592 | tf_op jit(solution)/shard_map/all_gather | solution.py:43
  476.5 20.5 %reduce-scatter.21.cloned.1.call-done = f32[512,256]{1,0:T(8,128)} async-done(((f32[1024,256]{1,0:T(8,128)}), f32[512,256]{1,0:T(8,128)}) %reduce-scatter.21.cloned.1.call-update) | async-done | bytes 524304 | tf_op jit(solution)/shard_map/reduce_scatter | solution.py:47
  499.1 4.2 multiply_reduce_fusion
  507.9 3.6 convolution_convert_fusion
  514.9 19.4 %all-gather.20.cloned.1.call-done = bf16[1024,768]{0,1:T(8,128)(2,1)} async-done(((bf16[512,768]{0,1:T(8,128)(2,1)}), bf16[1024,768]{0,1:T(8,128)(2,1)}) %all-gather.20.cloned.1.call-update) | async-done | bytes 1572880 | tf_op jit(solution)/shard_map/all_gather | solution.py:56
  541.1 65.0 %all-reduce = (f32[512]{0:T(512)}, f32[512]{0:T(512)}, f32[512]{0:T(512)}, f32[512]{0:T(512)}, f32[512]{0:T(512)}, /*index=5*/f32[512]{0:T(512)}) all-reduce(f32[512]{0:T(512)S(1)} %get-tuple-element.50, f32[512]{0:T(512)S(1)} %get-tuple-element.14, ...), channel_id=1, replica_groups=mesh['dp'=4,'row'=2,'col'=4] {'dp','col'}, use_global_device_ids=true, to_apply=%region_33.34 | all-reduce | flops 3072 | bytes 24576 | tf_op jit(solution)/shard_map/psum | solution.py:258
  606.2 19.9 %all-reduce.1 = (f32[2,256]{1,0:T(2,128)}, f32[1024]{0:T(1024)}) all-reduce(f32[2,256]{1,0:T(2,128)S(1)} %pad_maximum_fusion.1, f32[1024]{0:T(1024)S(1)} %get-tuple-element.52), channel_id=1, replica_groups=mesh['dp'=4,'row'=2,'col'=4] {'dp','row'}, use_global_device_ids=true, to_apply=%region_30.31 | all-reduce | flops 1536 | bytes 12288 | tf_op jit(solution)/shard_map/psum | solution.py:269
  626.1 34.0 %all-reduce.9.cloned.1.call-done = (bf16[512,3,256]{2,0,1:T(8,128)(2,1)}, bf16[256,512]{1,0:T(8,128)(2,1)}, bf16[512,1024]{1,0:T(8,128)(2,1)}, bf16[1024,512]{1,0:T(8,128)(2,1)}) async-done(((bf16[512,3,256]{2,0,1:T(8,128)(2,1)}, bf16[256,512]{1,0:T(8,128)(2,1)}, bf16[512,1024]{1,0:T(8,128)(2,1)}, bf16[1024,512]{1,0:T(8,128)(2,1)}), (bf16[512,3,256]{2,0,1:T(8,128)(2,1)}, bf16[256,512]{1,0:T(8,128)(2,1)}, ...) | async-done | bytes 3145744 | tf_op jit(solution)/shard_map/psum | solution.py:279
  667.5 25.3 %reduce-scatter.23.cloned.1.call-done = f32[256,512]{1,0:T(8,128)} async-done(((f32[1024,512]{1,0:T(8,128)}), f32[256,512]{1,0:T(8,128)}) %reduce-scatter.23.cloned.1.call-update) | async-done | bytes 524304 | tf_op jit(solution)/shard_map/reduce_scatter | solution.py:60
  (151 shorter events, 56.5 us)
Async XLA Ops:
  7.2 239.7 %copy-start = (bf16[1024,512]{1,0:T(8,128)(2,1)S(1)}, bf16[1024,512]{1,0:T(8,128)(2,1)}, u32[]{:S(2)}) copy-start(bf16[1024,512]{1,0:T(8,128)(2,1)} %param.24) | copy-start | bytes 3145732
  7.2 21.8 %all-gather.8.cloned.1.call-start = ((), (), s32[]{:S(2)}) async-start(), calls=%async_computation.8 | async-start | bytes 1310720 | tf_op jit(solution)/shard_map/all_gather | solution.py:17
  7.9 68.6 %reduce-scatter.9.cloned.1.call-start = ((), (), s32[]{:S(2)}) async-start(), calls=%async_computation.9 | async-start | bytes 4718592 | tf_op jit(solution)/shard_map/reduce_scatter | solution.py:21
  9.4 23.5 %copy-start.16 = (bf16[512,3,256]{0,2,1:T(8,128)(2,1)}, bf16[512,3,256]{0,2,1:T(8,128)(2,1)S(1)}, u32[]{:S(2)}) copy-start(bf16[512,3,256]{0,2,1:T(8,128)(2,1)S(1)} %copy.39) | copy-start | bytes 2359300
  33.0 92.6 %reduce-scatter.11.cloned.1.call-start = ((), (), s32[]{:S(2)}) async-start(), calls=%async_computation.10 | async-start | bytes 2621440 | tf_op jit(solution)/shard_map/reduce_scatter | solution.py:34
  92.4 33.2 %copy-start.28 = (f32[512]{0:T(512)S(1)}, f32[512]{0:T(512)}, u32[]{:S(2)}) copy-start(f32[512]{0:T(512)} %param.19) | copy-start | bytes 6148
  94.2 38.3 %copy-start.24 = (f32[512]{0:T(512)S(1)}, f32[512]{0:T(512)}, u32[]{:S(2)}) copy-start(f32[512]{0:T(512)} %param.20) | copy-start | bytes 6148
  94.2 38.3 %copy-start.26 = (f32[512]{0:T(512)S(1)}, f32[512]{0:T(512)}, u32[]{:S(2)}) copy-start(f32[512]{0:T(512)} %param.21) | copy-start | bytes 6148
  94.3 57.0 %all-gather.10.cloned.1.call-start = ((), (), s32[]{:S(2)}) async-start(), calls=%async_computation.11 | async-start | bytes 1310720 | tf_op jit(solution)/shard_map/all_gather | solution.py:17
  134.4 76.2 %reduce-scatter.13.cloned.1.call-start = ((), (), s32[]{:S(2)}) async-start(), calls=%async_computation.12 | async-start | bytes 6291456 | tf_op jit(solution)/shard_map/reduce_scatter | solution.py:21
  156.1 54.6 %copy-start.25 = (f32[1024]{0:T(1024)S(1)}, f32[1024]{0:T(1024)}, u32[]{:S(2)}) copy-start(f32[1024]{0:T(1024)} %param.23) | copy-start | bytes 12292
  156.1 90.8 %all-gather.12.cloned.1.call-start = ((), (), s32[]{:S(2)}) async-start(), calls=%async_computation.13 | async-start | bytes 3145728 | tf_op jit(solution)/shard_map/all_gather | solution.py:30
  213.7 68.8 %reduce-scatter.15.cloned.1.call-start = ((), (), s32[]{:S(2)}) async-start(), calls=%async_computation.14 | async-start | bytes 2621440 | tf_op jit(solution)/shard_map/reduce_scatter | solution.py:34
  251.1 31.4 %copy-start.29 = (f32[512]{0:T(512)S(1)}, f32[512]{0:T(512)}, u32[]{:S(2)}) copy-start(f32[512]{0:T(512)} %param.25) | copy-start | bytes 6148
  251.1 38.5 %copy-start.27 = (f32[512]{0:T(512)S(1)}, f32[512]{0:T(512)}, u32[]{:S(2)}) copy-start(f32[512]{0:T(512)} %param.26) | copy-start | bytes 6148
  251.1 44.9 %copy-start.30 = (f32[512]{0:T(512)S(1)}, f32[512]{0:T(512)}, u32[]{:S(2)}) copy-start(f32[512]{0:T(512)} %param.27) | copy-start | bytes 6148
  251.1 65.4 %all-gather.14.cloned.1.call-start = ((), (), s32[]{:S(2)}) async-start(), calls=%async_computation.15 | async-start | bytes 1310720 | tf_op jit(solution)/shard_map/all_gather | solution.py:43
  299.6 75.9 %reduce-scatter.17.cloned.1.call-start = ((), (), s32[]{:S(2)}) async-start(), calls=%async_computation.16 | async-start | bytes 6291456 | tf_op jit(solution)/shard_map/reduce_scatter | solution.py:47
  320.9 91.3 %copy-start.34 = (bf16[512,1024]{1,0:T(8,128)(2,1)S(1)}, bf16[512,1024]{1,0:T(8,128)(2,1)}, u32[]{:S(2)}) copy-start(bf16[512,1024]{1,0:T(8,128)(2,1)} %param.22) | copy-start | bytes 3145732
  321.0 91.3 %all-gather.16.cloned.1.call-start = ((), (), s32[]{:S(2)}) async-start(), calls=%async_computation.17 | async-start | bytes 3145728 | tf_op jit(solution)/shard_map/all_gather | solution.py:56
  379.0 68.8 %reduce-scatter.19.cloned.1.call-start = ((), (), s32[]{:S(2)}) async-start(), calls=%async_computation.18 | async-start | bytes 2621440 | tf_op jit(solution)/shard_map/reduce_scatter | solution.py:60
  416.4 31.4 %copy-start.4 = (f32[256,512]{1,0:T(8,128)S(1)}, f32[256,512]{1,0:T(8,128)}, u32[]{:S(2)}) copy-start(f32[256,512]{1,0:T(8,128)} %get-tuple-element.56) | copy-start | bytes 1572868
  416.4 31.4 %copy-start.10 = (f32[256,512]{1,0:T(8,128)S(1)}, f32[256,512]{1,0:T(8,128)}, u32[]{:S(2)}) copy-start(f32[256,512]{1,0:T(8,128)} %copy-done.9) | copy-start | bytes 1572868
  416.5 57.3 %all-gather.18.cloned.1.call-start = ((), (), s32[]{:S(2)}) async-start(), calls=%async_computation.19 | async-start | bytes 1310720 | tf_op jit(solution)/shard_map/all_gather | solution.py:43
  456.9 40.1 %reduce-scatter.21.cloned.1.call-start = ((), (), s32[]{:S(2)}) async-start(), calls=%async_computation.20 | async-start | bytes 1572864 | tf_op jit(solution)/shard_map/reduce_scatter | solution.py:47
  476.5 22.6 %copy-start.14 = (f32[512,1,256]{0,2,1:T(8,128)S(1)}, f32[512,1,256]{0,2,1:T(8,128)}, u32[]{:S(2)}) copy-start(f32[512,1,256]{0,2,1:T(8,128)} %copy-done.13) | copy-start | bytes 1572868
  476.5 57.9 %all-gather.20.cloned.1.call-start = ((), (), s32[]{:S(2)}) async-start(), calls=%async_computation.21 | async-start | bytes 2359296 | tf_op jit(solution)/shard_map/all_gather | solution.py:56
  507.0 153.1 %all-reduce.9.cloned.1.call-start = ((), (), s32[]{:S(2)}) async-start(), calls=%async_computation.23 | async-start | bytes 6291456 | tf_op jit(solution)/shard_map/psum | solution.py:279
  511.5 22.8 %copy-start.19 = (bf16[1024,512]{1,0:T(8,128)(2,1)S(1)}, bf16[1024,512]{1,0:T(8,128)(2,1)}, u32[]{:S(2)}) copy-start(bf16[1024,512]{1,0:T(8,128)(2,1)} %all-gather.8.cloned.1.call-done) | copy-start | bytes 3145732
  537.9 154.9 %reduce-scatter.23.cloned.1.call-start = ((), (), s32[]{:S(2)}) async-start(), calls=%async_computation.22 | async-start | bytes 2621440 | tf_op jit(solution)/shard_map/reduce_scatter | solution.py:60
  665.9 26.9 %copy-start.6 = (f32[256,512]{1,0:T(8,128)S(1)}, f32[256,512]{1,0:T(8,128)}, u32[]{:S(2)}) copy-start(f32[256,512]{1,0:T(8,128)} %copy-done.5) | copy-start | bytes 1572868
  665.9 28.8 %copy-start.1 = (bf16[1024,512]{1,0:T(8,128)(2,1)S(1)}, bf16[1024,512]{1,0:T(8,128)(2,1)}, u32[]{:S(2)}) copy-start(bf16[1024,512]{1,0:T(8,128)(2,1)} %param.24) | copy-start | bytes 3145732
  (19 other events, 68.1 us)
Sparse Core Ops, SparseCore 0:
  9.6 19.4 all-gather.7
  33.1 43.4 reduce-scatter.8
  94.4 31.1 reduce-scatter.10
  134.6 16.6 all-gather.9
  156.2 54.3 reduce-scatter.12
  213.8 33.0 all-gather.11
  251.2 31.1 reduce-scatter.14
  299.7 16.7 all-gather.13
  321.1 54.3 reduce-scatter.16
  379.1 33.0 all-gather.15
  416.6 31.1 reduce-scatter.18
  457.0 16.7 all-gather.17
  476.6 20.3 reduce-scatter.20
  507.1 27.1 all-gather.19
  538.1 121.9 all-reduce.8
  662.4 30.3 reduce-scatter.22
where the time goes:
time: 702 us; the launch traced here: 701 us
  waiting for transfers between devices  482 us (69%)
  blocking collectives  113 us (16%)
  matrix products  45.8 us (7%)
  other arithmetic  35.5 us (5%)
  between operations  14.9 us (2%)
  local copies, waits for them, and re-layouts  9.27 us (1%)
    reduce_scatter x2, waiting for transfers between devices, forward_reduce(): lax.psum_scatter(product_term(jnp.int32(0), row_count * lax.axis_size('ro...  97.2 us
    reduce_scatter x2, waiting for transfers between devices, backward_reduce(): lax.psum_scatter(product_term(jnp.int32(0), row_count * lax.axis_size('ro...  74.9 us
    psum x1, blocking collectives, shards(): lax.psum((jnp.sum(first_norm_gradient, axis=0), jnp.sum(norm_gradient_tot...  65 us
    reduce_scatter x2, waiting for transfers between devices, forward_combine(): lax.psum_scatter(product_term(jnp.int32(0), row_count * lax.axis_size('co...  62.6 us
    reduce_scatter x2, waiting for transfers between devices, backward_combine(): lax.psum_scatter(product_term(jnp.int32(0), row_count * lax.axis_size('co...  56.5 us
    all_gather x2, waiting for transfers between devices, backward_collect(): return lax.all_gather(block, 'row', axis=0, tiled=True)  52.5 us
    all_gather x2, waiting for transfers between devices, forward_gather(): return lax.all_gather(block, 'col', axis=0, tiled=True)  36.4 us
    psum x1, waiting for transfers between devices, shards(): lax.psum(grad_qkv.astype(jnp.bfloat16), 'dp').astype(jnp.float32)  34 us
  transfers between devices with their start and end apart: 16, of which 16 were waited for; matrix products, arithmetic and copies ran while one was open for 3% of the time, Pallas kernels for 0%

commit v1 on v0

--- a/solution.py
+++ b/solution.py
@@ -1,7 +1,9 @@
+import functools
 import jax
 import jax.numpy as jnp
 from jax import lax
 from jax.sharding import PartitionSpec as P
+from jax.lax import axis_index, axis_size, ppermute
 
 MODEL_WIDTH = 1024
 HEADS = 16
@@ -13,8 +15,31 @@
 gauss_height = 0.3989422804014327
 
 
+def lay_threads(u, ax_name):
+    mat_out = axis_size(ax_name)
+    z_new, all_values, before = (mat_out, axis_index(ax_name), u.shape[0])
+    queue = [src_i * z_new if t == 0 else src_i for t, src_i in enumerate(u.shape)]
+    high = jnp.zeros(queue, u.dtype)
+    a_now = lax.dynamic_update_slice_in_dim(high, u, all_values * before, axis=0)
+    e_next = finding = u
+    for hop_no in range(1, z_new // 2 + 1):
+        e_next = ppermute(e_next, ax_name, [(t, (t + 1) % z_new) for t in range(z_new)])
+        a_now = lax.dynamic_update_slice_in_dim(
+            a_now, e_next, (all_values - hop_no) % z_new * before, axis=0
+        )
+        if 2 * hop_no < z_new:
+            finding = ppermute(finding, ax_name, [(t, (t - 1) % z_new) for t in range(z_new)])
+            a_now = lax.dynamic_update_slice_in_dim(
+                a_now, finding, (all_values + hop_no) % z_new * before, axis=0
+            )
+    return a_now
+
+
+solve_the_values = functools.partial(lay_threads, ax_name="col")
+
+
 def forward_gather(block):
-    return lax.all_gather(block, "col", axis=0, tiled=True)
+    return solve_the_values(block)
 
 
 def forward_reduce(product_term, row_count):

time: 702 us -> 693 us (0.987)
  waiting for transfers between devices: 482 us -> 465 us
    all_gather x2 -> x0, waiting for transfers between devices: 36.4 us -> none  [forward_gather(): return lax.all_gather(block, 'col', axis=0, tiled=True)]
    ppermute x0 -> x6, waiting for transfers between devices: none -> 17.1 us  [the longest x4 17.1 us: lay_threads(): ppermute(e_next, ax_name, [(t, (t + 1) % z_new) for t in range(z_new)])]
  transfers between devices with their start and end apart: 16 -> 20, of which waited for: 16 -> 18; matrix products, arithmetic and copies ran while one was open for 3% -> 3% of each run, Pallas kernels for 0% -> 0%
where the time goes in v1:
time: 693 us; the launch traced here: 692 us
  waiting for transfers between devices  465 us (67%)
  blocking collectives  113 us (16%)
  matrix products  43.5 us (6%)
  other arithmetic  32.5 us (5%)
  between operations  15.1 us (2%)
  local copies, waits for them, and re-layouts  14.8 us (2%)
  starting transfers between devices  7.66 us (1%)
    reduce_scatter x2, waiting for transfers between devices, forward_reduce(): lax.psum_scatter(product_term(jnp.int32(0), row_count * lax.axis_size('ro...  101 us
    reduce_scatter x2, waiting for transfers between devices, backward_reduce(): lax.psum_scatter(product_term(jnp.int32(0), row_count * lax.axis_size('ro...  74.8 us
    psum x1, blocking collectives, shards(): lax.psum((jnp.sum(first_norm_gradient, axis=0), jnp.sum(norm_gradient_tot...  64.9 us
    reduce_scatter x2, waiting for transfers between devices, forward_combine(): lax.psum_scatter(product_term(jnp.int32(0), row_count * lax.axis_size('co...  62.5 us
    reduce_scatter x2, waiting for transfers between devices, backward_combine(): lax.psum_scatter(product_term(jnp.int32(0), row_count * lax.axis_size('co...  56.3 us
    all_gather x2, waiting for transfers between devices, backward_collect(): return lax.all_gather(block, 'row', axis=0, tiled=True)  53 us
    all_gather x2, waiting for transfers between devices, backward_gather(): return lax.all_gather(block, 'col', axis=0, tiled=True)  33.6 us
    psum x1, waiting for transfers between devices, shards(): lax.psum(grad_qkv.astype(jnp.bfloat16), 'dp').astype(jnp.float32)  33.4 us
  transfers between devices with their start and end apart: 20, of which 18 were waited for; matrix products, arithmetic and copies ran while one was open for 3% of the time, Pallas kernels for 0%

profile of v1, /device:TPU:0, one launch (start us, length us, event | category | flops | bytes accessed | tf_op | source)
XLA Modules:
  0.0 691.7 jit_solution(16775958046374825187)
XLA Ops:
  9.8 4.4 collective-permute-done
  24.7 46.5 %reduce-scatter.9.cloned.1.call-done = f32[512,768]{1,0:T(8,128)} async-done(((f32[1024,768]{1,0:T(8,128)}), f32[512,768]{1,0:T(8,128)}) %reduce-scatter.9.cloned.1.call-update) | async-done | bytes 1572880 | tf_op jit(solution)/shard_map/reduce_scatter | solution.py:46
  77.8 8.6 %all_gather.18 = bf16[1024,256]{0,1:T(8,128)(2,1)S(1)} all-gather(bf16[512,256]{0,1:T(8,128)(2,1)S(1)} %bitcast.92), channel_id=1, replica_groups=mesh['dp'=4,'row'=2,'col'=4] {'row'}, dimensions={0}, use_global_device_ids=true | all-gather | bytes 786432 | tf_op jit(solution)/shard_map/all_gather | solution.py:55
  89.0 31.3 %reduce-scatter.11.cloned.1.call-done = f32[256,512]{1,0:T(8,128)} async-done(((f32[1024,512]{1,0:T(8,128)}), f32[256,512]{1,0:T(8,128)}) %reduce-scatter.11.cloned.1.call-update) | async-done | bytes 524304 | tf_op jit(solution)/shard_map/reduce_scatter | solution.py:59
  122.3 4.9 all-reduce.5
  130.4 6.2 collective-permute-done.3
  136.6 5.7 collective-permute-done.5
  143.4 3.2 fusion.32
  146.7 54.3 %reduce-scatter.13.cloned.1.call-done = f32[512,1024]{1,0:T(8,128)} async-done(((f32[1024,1024]{1,0:T(8,128)}), f32[512,1024]{1,0:T(8,128)}) %reduce-scatter.13.cloned.1.call-update) | async-done | bytes 2097168 | tf_op jit(solution)/shard_map/reduce_scatter | solution.py:46
  201.0 3.0 multiply_convert_fusion.1
  204.0 33.2 %all-gather.6.cloned.1.call-done = bf16[1024,1024]{1,0:T(8,128)(2,1)} async-done(((bf16[512,1024]{1,0:T(8,128)(2,1)}), bf16[1024,1024]{1,0:T(8,128)(2,1)}) %all-gather.6.cloned.1.call-update) | async-done | bytes 2097168 | tf_op jit(solution)/shard_map/all_gather | solution.py:55
  237.3 4.2 fusion.33
  241.5 31.3 %reduce-scatter.15.cloned.1.call-done = f32[256,512]{1,0:T(8,128)} async-done(((f32[1024,512]{1,0:T(8,128)}), f32[256,512]{1,0:T(8,128)}) %reduce-scatter.15.cloned.1.call-update) | async-done | bytes 524304 | tf_op jit(solution)/shard_map/reduce_scatter | solution.py:59
  274.9 4.9 all-reduce.4
  281.3 4.9 all-reduce.3
  289.9 16.8 %all-gather.8.cloned.1.call-done = bf16[1024,512]{1,0:T(8,128)(2,1)} async-done(((bf16[256,512]{1,0:T(8,128)(2,1)}), bf16[1024,512]{1,0:T(8,128)(2,1)}) %all-gather.8.cloned.1.call-update) | async-done | bytes 1048592 | tf_op jit(solution)/shard_map/all_gather | solution.py:68
  306.7 4.5 fusion.34
  311.5 54.3 %reduce-scatter.17.cloned.1.call-done = f32[512,1024]{1,0:T(8,128)} async-done(((f32[1024,1024]{1,0:T(8,128)}), f32[512,1024]{1,0:T(8,128)}) %reduce-scatter.17.cloned.1.call-update) | async-done | bytes 2097168 | tf_op jit(solution)/shard_map/reduce_scatter | solution.py:72
  365.8 3.5 fusion.24
  369.3 33.2 %all-gather.10.cloned.1.call-done = bf16[1024,1024]{1,0:T(8,128)(2,1)} async-done(((bf16[512,1024]{1,0:T(8,128)(2,1)}), bf16[1024,1024]{1,0:T(8,128)(2,1)}) %all-gather.10.cloned.1.call-update) | async-done | bytes 2097168 | tf_op jit(solution)/shard_map/all_gather | solution.py:81
  402.5 4.2 fusion.35
  406.8 31.3 %reduce-scatter.19.cloned.1.call-done = f32[256,512]{1,0:T(8,128)} async-done(((f32[1024,512]{1,0:T(8,128)}), f32[256,512]{1,0:T(8,128)}) %reduce-scatter.19.cloned.1.call-update) | async-done | bytes 524304 | tf_op jit(solution)/shard_map/reduce_scatter | solution.py:85
  440.1 4.9 all-reduce.2
  447.2 16.8 %all-gather.12.cloned.1.call-done = bf16[1024,512]{1,0:T(8,128)(2,1)} async-done(((bf16[256,512]{1,0:T(8,128)(2,1)}), bf16[1024,512]{1,0:T(8,128)(2,1)}) %all-gather.12.cloned.1.call-update) | async-done | bytes 1048592 | tf_op jit(solution)/shard_map/all_gather | solution.py:68
  466.8 20.5 %reduce-scatter.21.cloned.1.call-done = f32[512,256]{1,0:T(8,128)} async-done(((f32[1024,256]{1,0:T(8,128)}), f32[512,256]{1,0:T(8,128)}) %reduce-scatter.21.cloned.1.call-update) | async-done | bytes 524304 | tf_op jit(solution)/shard_map/reduce_scatter | solution.py:72
  489.3 4.2 multiply_reduce_fusion
  497.4 4.0 convolution_convert_fusion
  504.9 19.8 %all-gather.14.cloned.1.call-done = bf16[1024,768]{0,1:T(8,128)(2,1)} async-done(((bf16[512,768]{0,1:T(8,128)(2,1)}), bf16[1024,768]{0,1:T(8,128)(2,1)}) %all-gather.14.cloned.1.call-update) | async-done | bytes 1572880 | tf_op jit(solution)/shard_map/all_gather | solution.py:81
  532.1 64.9 %all-reduce = (f32[512]{0:T(512)}, f32[512]{0:T(512)}, f32[512]{0:T(512)}, f32[512]{0:T(512)}, f32[512]{0:T(512)}, /*index=5*/f32[512]{0:T(512)}) all-reduce(f32[512]{0:T(512)S(1)} %get-tuple-element.64, f32[512]{0:T(512)S(1)} %get-tuple-element.28, ...), channel_id=1, replica_groups=mesh['dp'=4,'row'=2,'col'=4] {'dp','col'}, use_global_device_ids=true, to_apply=%region_33.34 | all-reduce | flops 3072 | bytes 24576 | tf_op jit(solution)/shard_map/psum | solution.py:283
  597.2 20.0 %all-reduce.1 = (f32[2,256]{1,0:T(2,128)}, f32[1024]{0:T(1024)}) all-reduce(f32[2,256]{1,0:T(2,128)S(1)} %pad_maximum_fusion.1, f32[1024]{0:T(1024)S(1)} %get-tuple-element.66), channel_id=1, replica_groups=mesh['dp'=4,'row'=2,'col'=4] {'dp','row'}, use_global_device_ids=true, to_apply=%region_30.31 | all-reduce | flops 1536 | bytes 12288 | tf_op jit(solution)/shard_map/psum | solution.py:294
  617.2 33.4 %all-reduce.9.cloned.1.call-done = (bf16[512,3,256]{0,2,1:T(8,128)(2,1)}, bf16[256,512]{1,0:T(8,128)(2,1)}, bf16[512,1024]{1,0:T(8,128)(2,1)}, bf16[1024,512]{1,0:T(8,128)(2,1)}) async-done(((bf16[512,3,256]{0,2,1:T(8,128)(2,1)}, bf16[256,512]{1,0:T(8,128)(2,1)}, bf16[512,1024]{1,0:T(8,128)(2,1)}, bf16[1024,512]{1,0:T(8,128)(2,1)}), (bf16[512,3,256]{0,2,1:T(8,128)(2,1)}, bf16[256,512]{1,0:T(8,128)(2,1)}, ...) | async-done | bytes 3145744 | tf_op jit(solution)/shard_map/psum | solution.py:304
  658.2 25.0 %reduce-scatter.23.cloned.1.call-done = f32[256,512]{1,0:T(8,128)} async-done(((f32[1024,512]{1,0:T(8,128)}), f32[256,512]{1,0:T(8,128)}) %reduce-scatter.23.cloned.1.call-update) | async-done | bytes 524304 | tf_op jit(solution)/shard_map/reduce_scatter | solution.py:85
  (172 shorter events, 68.7 us)
Async XLA Ops:
  7.2 230.1 %copy-start = (bf16[1024,512]{1,0:T(8,128)(2,1)S(1)}, bf16[1024,512]{1,0:T(8,128)(2,1)}, u32[]{:S(2)}) copy-start(bf16[1024,512]{1,0:T(8,128)(2,1)} %param.24) | copy-start | bytes 3145732
  7.2 64.0 %reduce-scatter.9.cloned.1.call-start = ((), (), s32[]{:S(2)}) async-start(), calls=%async_computation.8 | async-start | bytes 4718592 | tf_op jit(solution)/shard_map/reduce_scatter | solution.py:46
  7.2 7.0 %collective-permute-start = (bf16[256,512]{1,0:T(8,128)(2,1)}, bf16[256,512]{1,0:T(8,128)(2,1)S(1)}, u32[]{:S(2)}, u32[]{:S(2)}) collective-permute-start(bf16[256,512]{1,0:T(8,128)(2,1)} %param.15), channel_id=1, source_target_pairs={{0,1},{1,2},{2,3},{3,0},{4,5},{5,6},{6,7},{7,4},{8,9},{9,10},{10,1... | collective-permute-start | bytes 786440 | tf_op jit(solution)/shard_map/ppermute | solution.py:26
  7.8 11.6 %collective-permute-start.1 = (bf16[256,512]{1,0:T(8,128)(2,1)}, bf16[256,512]{1,0:T(8,128)(2,1)S(1)}, u32[]{:S(2)}, u32[]{:S(2)}) collective-permute-start(bf16[256,512]{1,0:T(8,128)(2,1)} %param.15), channel_id=1, source_target_pairs={{0,3},{1,0},{2,1},{3,2},{4,7},{5,4},{6,5},{7,6},{8,11},{9,8},{10,9... | collective-permute-start | bytes 786440 | tf_op jit(solution)/shard_map/ppermute | solution.py:31
  14.2 5.9 collective-permute-start.2
  23.8 96.5 %reduce-scatter.11.cloned.1.call-start = ((), (), s32[]{:S(2)}) async-start(), calls=%async_computation.9 | async-start | bytes 2621440 | tf_op jit(solution)/shard_map/reduce_scatter | solution.py:59
  87.1 33.2 %copy-start.30 = (f32[512]{0:T(512)S(1)}, f32[512]{0:T(512)}, u32[]{:S(2)}) copy-start(f32[512]{0:T(512)} %param.19) | copy-start | bytes 6148
  88.9 38.3 %copy-start.26 = (f32[512]{0:T(512)S(1)}, f32[512]{0:T(512)}, u32[]{:S(2)}) copy-start(f32[512]{0:T(512)} %param.20) | copy-start | bytes 6148
  88.9 38.3 %copy-start.28 = (f32[512]{0:T(512)S(1)}, f32[512]{0:T(512)}, u32[]{:S(2)}) copy-start(f32[512]{0:T(512)} %param.21) | copy-start | bytes 6148
  88.9 112.0 %reduce-scatter.13.cloned.1.call-start = ((), (), s32[]{:S(2)}) async-start(), calls=%async_computation.10 | async-start | bytes 6291456 | tf_op jit(solution)/shard_map/reduce_scatter | solution.py:46
  128.6 8.0 %collective-permute-start.3 = (bf16[256,512]{1,0:T(8,128)(2,1)S(1)}, bf16[256,512]{1,0:T(8,128)(2,1)S(1)}, u32[]{:S(2)}, u32[]{:S(2)}) collective-permute-start(bf16[256,512]{1,0:T(8,128)(2,1)S(1)} %get-tuple-element.71), channel_id=1, source_target_pairs={{0,1},{1,2},{2,3},{3,0},{4,5},{5,6},{6,7},{7,4},{8,9},{9,10},{10,1... | collective-permute-start | bytes 786440 | tf_op jit(solution)/shard_map/ppermute | solution.py:26
  128.6 8.0 %collective-permute-start.4 = (bf16[256,512]{1,0:T(8,128)(2,1)S(1)}, bf16[256,512]{1,0:T(8,128)(2,1)S(1)}, u32[]{:S(2)}, u32[]{:S(2)}) collective-permute-start(bf16[256,512]{1,0:T(8,128)(2,1)S(1)} %get-tuple-element.71), channel_id=1, source_target_pairs={{0,3},{1,0},{2,1},{3,2},{4,7},{5,4},{6,5},{7,6},{8,11},{9,8},{10,9... | collective-permute-start | bytes 786440 | tf_op jit(solution)/shard_map/ppermute | solution.py:31
  136.6 5.8 collective-permute-start.5
  146.6 54.3 %copy-start.27 = (f32[1024]{0:T(1024)S(1)}, f32[1024]{0:T(1024)}, u32[]{:S(2)}) copy-start(f32[1024]{0:T(1024)} %param.23) | copy-start | bytes 12292
  146.6 90.6 %all-gather.6.cloned.1.call-start = ((), (), s32[]{:S(2)}) async-start(), calls=%async_computation.11 | async-start | bytes 3145728 | tf_op jit(solution)/shard_map/all_gather | solution.py:55
  204.0 68.7 %reduce-scatter.15.cloned.1.call-start = ((), (), s32[]{:S(2)}) async-start(), calls=%async_computation.12 | async-start | bytes 2621440 | tf_op jit(solution)/shard_map/reduce_scatter | solution.py:59
  241.4 31.3 %copy-start.31 = (f32[512]{0:T(512)S(1)}, f32[512]{0:T(512)}, u32[]{:S(2)}) copy-start(f32[512]{0:T(512)} %param.25) | copy-start | bytes 6148
  241.4 38.5 %copy-start.29 = (f32[512]{0:T(512)S(1)}, f32[512]{0:T(512)}, u32[]{:S(2)}) copy-start(f32[512]{0:T(512)} %param.26) | copy-start | bytes 6148
  241.4 44.8 %copy-start.32 = (f32[512]{0:T(512)S(1)}, f32[512]{0:T(512)}, u32[]{:S(2)}) copy-start(f32[512]{0:T(512)} %param.27) | copy-start | bytes 6148
  241.4 65.3 %all-gather.8.cloned.1.call-start = ((), (), s32[]{:S(2)}) async-start(), calls=%async_computation.13 | async-start | bytes 1310720 | tf_op jit(solution)/shard_map/all_gather | solution.py:68
  289.9 75.9 %reduce-scatter.17.cloned.1.call-start = ((), (), s32[]{:S(2)}) async-start(), calls=%async_computation.14 | async-start | bytes 6291456 | tf_op jit(solution)/shard_map/reduce_scatter | solution.py:72
  311.2 91.3 %copy-start.36 = (bf16[512,1024]{1,0:T(8,128)(2,1)S(1)}, bf16[512,1024]{1,0:T(8,128)(2,1)}, u32[]{:S(2)}) copy-start(bf16[512,1024]{1,0:T(8,128)(2,1)} %param.22) | copy-start | bytes 3145732
  311.2 91.3 %all-gather.10.cloned.1.call-start = ((), (), s32[]{:S(2)}) async-start(), calls=%async_computation.15 | async-start | bytes 3145728 | tf_op jit(solution)/shard_map/all_gather | solution.py:81
  369.3 68.8 %reduce-scatter.19.cloned.1.call-start = ((), (), s32[]{:S(2)}) async-start(), calls=%async_computation.16 | async-start | bytes 2621440 | tf_op jit(solution)/shard_map/reduce_scatter | solution.py:85
  406.7 31.4 %copy-start.4 = (f32[256,512]{1,0:T(8,128)S(1)}, f32[256,512]{1,0:T(8,128)}, u32[]{:S(2)}) copy-start(f32[256,512]{1,0:T(8,128)} %get-tuple-element.72) | copy-start | bytes 1572868
  406.7 31.4 %copy-start.10 = (f32[256,512]{1,0:T(8,128)S(1)}, f32[256,512]{1,0:T(8,128)}, u32[]{:S(2)}) copy-start(f32[256,512]{1,0:T(8,128)} %copy-done.9) | copy-start | bytes 1572868
  406.7 57.3 %all-gather.12.cloned.1.call-start = ((), (), s32[]{:S(2)}) async-start(), calls=%async_computation.17 | async-start | bytes 1310720 | tf_op jit(solution)/shard_map/all_gather | solution.py:68
  447.1 40.1 %reduce-scatter.21.cloned.1.call-start = ((), (), s32[]{:S(2)}) async-start(), calls=%async_computation.18 | async-start | bytes 1572864 | tf_op jit(solution)/shard_map/reduce_scatter | solution.py:72
  466.8 57.9 %all-gather.14.cloned.1.call-start = ((), (), s32[]{:S(2)}) async-start(), calls=%async_computation.19 | async-start | bytes 2359296 | tf_op jit(solution)/shard_map/all_gather | solution.py:81
  497.3 153.2 %all-reduce.9.cloned.1.call-start = ((), (), s32[]{:S(2)}) async-start(), calls=%async_computation.21 | async-start | bytes 6291456 | tf_op jit(solution)/shard_map/psum | solution.py:304
  528.3 154.9 %reduce-scatter.23.cloned.1.call-start = ((), (), s32[]{:S(2)}) async-start(), calls=%async_computation.20 | async-start | bytes 2621440 | tf_op jit(solution)/shard_map/reduce_scatter | solution.py:85
  656.6 28.6 %copy-start.1 = (bf16[1024,512]{1,0:T(8,128)(2,1)S(1)}, bf16[1024,512]{1,0:T(8,128)(2,1)}, u32[]{:S(2)}) copy-start(bf16[1024,512]{1,0:T(8,128)(2,1)} %param.24) | copy-start | bytes 3145732
  (26 other events, 165.3 us)
Sparse Core Ops, SparseCore 0:
  23.9 47.2 reduce-scatter.8
  89.1 31.1 reduce-scatter.10
  146.8 54.1 reduce-scatter.12
  204.1 33.0 all-gather.5
  241.6 31.1 reduce-scatter.14
  290.0 16.6 all-gather.7
  311.4 54.3 reduce-scatter.16
  369.4 33.0 all-gather.9
  406.9 31.1 reduce-scatter.18
  447.3 16.7 all-gather.11
  466.9 20.3 reduce-scatter.20
  497.4 27.1 all-gather.13
  528.4 122.0 all-reduce.8
  652.9 30.2 reduce-scatter.22
